TPU v7x, 256 devices: a whole 4x4x8 slice. The times are simulated.
256 devices in a mesh: row: 32 (over z_hi, x, core), col: 8 (over z_lo, y).
Axes of the slice: x: 4, y: 4, z: 8 (z_hi: 4, z_lo: 2; z = z_hi * 2 + z_lo), core: 2. Of those that a mesh axis runs over, the one named last changes fastest.
Arguments:
- density_factor: bfloat16 [6144, 512], P('row', 'col'), may hold values from -0.25 to 0.25
- hole_factor: bfloat16 [6144, 512], P('row', 'col'), may hold values from -0.25 to 0.25
- ph_factor: bfloat16 [6144, 512], P('row', 'col'), may hold values from -0.25 to 0.25
- hamiltonian: bfloat16 [6144, 6144], P('row', 'col'), as said below
- multiplier_q: bfloat16 [6144, 6144], P('row', 'col'), as said below
- multiplier_g: bfloat16 [6144, 6144], P('row', 'col'), as said below
- ph_perm: int32 [6144], replicated, may hold values from 0 to 6143, as said below
- block_lengths: int32 [48], replicated, may hold values from 1 to 256, 6144 in all
Outputs:
- grad_density: float32 [6144, 512], P('row', 'col')
- grad_hole: float32 [6144, 512], P('row', 'col')
- grad_ph: float32 [6144, 512], P('row', 'col')
Inputs may be any that keep to these rules, and one draw needn't show every extreme that they name: `ph_perm`: a permutation of the rows; each aligned block of 192 entries holds exactly 6 values from each aligned range of 192 rows. `block_lengths`: the lengths sum to 6144. `hamiltonian`: symmetric. `multiplier_q`: symmetric. `multiplier_g`: symmetric.
All inputs are finite; a program needn't handle non-finite values.
Results may differ from a plain program's by a relative error of at most 0.00035.
The roundings to bfloat16 on the way count: a program that leaves them out, or rounds other values in their place, can miss the bound.
Values may be sent and summed in bfloat16 or wider, within the bound.
No kernel may reach another device: no remote copies, remote signals or barrier semaphores. Data moves between devices by JAX's collectives and lax.ppermute only.
A program may use at most 64 MiB of HBM per device.

v0:
```python
import jax
import jax.numpy as jnp
from jax import lax
from jax.sharding import PartitionSpec as P

shift_value = 2.0
penalty = 2.5


def block_means(values, lengths):
    offsets = jnp.cumsum(lengths)
    positions = jnp.arange(values.shape[0], dtype=jnp.int32)
    segment = jnp.sum((positions[:, None] >= offsets[None, :]).astype(jnp.int32), axis=1)
    member = (segment[:, None] == jnp.arange(lengths.shape[0], dtype=jnp.int32)[None, :]).astype(
        jnp.float32
    )
    means = jnp.sum(member * values[:, None], axis=0) / lengths.astype(jnp.float32)
    return jnp.sum(member * means[None, :], axis=1)


def contract_rows(left, right):
    return lax.dot_general(
        left, right, (((1,), (1,)), ((), ())), preferred_element_type=jnp.float32
    )


def local(
    density_factor,
    hole_factor,
    ph_factor,
    hamiltonian,
    multiplier_q,
    multiplier_g,
    ph_perm,
    block_lengths,
):
    groups = lax.axis_size("row")
    row_index = lax.axis_index("row")
    col_index = lax.axis_index("col")
    block = density_factor.shape[0]
    rank_part = density_factor.shape[1]
    width = multiplier_q.shape[1]
    sends = block // groups
    row_ids = row_index * block + jnp.arange(block, dtype=jnp.int32)
    col_ids = col_index * width + jnp.arange(width, dtype=jnp.int32)
    on_diag = row_ids[:, None] == col_ids[None, :]
    density_sq = jnp.sum(jnp.square(density_factor.astype(jnp.float32)), axis=1)
    ph_sq = jnp.sum(jnp.square(ph_factor.astype(jnp.float32)), axis=1)
    mult_diag = jnp.sum(jnp.where(on_diag, multiplier_g.astype(jnp.float32), 0.0), axis=1)
    density_sq, ph_sq, mult_diag = lax.psum((density_sq, ph_sq, mult_diag), "col")
    density_all, ph_all, mult_all = (
        lax.all_gather(density_sq, "row", axis=0, tiled=True),
        lax.all_gather(ph_sq, "row", axis=0, tiled=True),
        lax.all_gather(mult_diag, "row", axis=0, tiled=True),
    )
    shifted = 2.0 * block_means(density_all, block_lengths)
    shifted_ph = jnp.take(shifted, ph_perm)
    weight_diag = mult_all + penalty * (shifted_ph - jnp.take(density_all, ph_perm) - ph_all)
    weight_pair = jnp.zeros_like(weight_diag).at[ph_perm].set(weight_diag)
    scaling = 2.0 * block_means(weight_pair, block_lengths)
    scale_rows = lax.dynamic_slice_in_dim(scaling, row_index * block, block)
    shift_rows = lax.dynamic_slice_in_dim(shifted_ph, row_index * block, block)
    table = ph_perm.reshape(groups, block)
    source = table // block
    mine = lax.dynamic_index_in_dim(source, row_index, 0, keepdims=False)
    member = (mine[:, None] == jnp.arange(groups, dtype=jnp.int32)[None, :]).astype(jnp.int32)
    earlier = jnp.cumsum(member, axis=0) - member
    slot = mine * sends + jnp.sum(earlier * member, axis=1)
    slot_back = jnp.argsort(slot)
    position = jnp.arange(block, dtype=jnp.int32)[None, :]
    ranked = jnp.where(source == row_index, position, block + position)
    chosen = jnp.argsort(ranked, axis=1)[:, :sends]
    anchor = (jnp.take_along_axis(table, chosen, axis=1) - row_index * block).reshape(block)
    anchor_back = jnp.argsort(anchor)
    pair_local = jnp.concatenate([density_factor, hole_factor], axis=1)
    outgoing = jnp.take(density_factor, anchor, axis=0)
    incoming = lax.all_to_all(outgoing, "row", split_axis=0, concat_axis=0, tiled=True)
    density_ph = jnp.take(incoming, slot, axis=0)
    ph_local = jnp.concatenate([density_ph, ph_factor], axis=1)
    pair_whole, ph_whole = (
        lax.all_gather(pair_local, "row", axis=0, tiled=True),
        lax.all_gather(ph_local, "row", axis=0, tiled=True),
    )
    pair_rows = pair_whole
    ph_rows = ph_whole
    gram_cols = lax.psum_scatter(
        jnp.concatenate(
            [contract_rows(pair_rows, pair_local), contract_rows(ph_rows, ph_local)], axis=1
        ),
        "col",
        scatter_dimension=0,
        tiled=True,
    )
    resid_q = jnp.where(on_diag, shift_value, 0.0) - gram_cols[:, :block].T
    resid_g = jnp.where(on_diag, shift_rows[:, None], 0.0) - gram_cols[:, block:].T
    weight_q = (multiplier_q.astype(jnp.float32) + penalty * resid_q).astype(jnp.bfloat16)
    weight_g = (multiplier_g.astype(jnp.float32) + penalty * resid_g).astype(jnp.bfloat16)
    weight_q, weight_g = (weight_q, weight_g)
    pair_rows = pair_whole
    ph_rows = ph_whole
    energy = jnp.dot(
        lax.all_gather(hamiltonian, "col", axis=1, tiled=True),
        pair_rows[:, :rank_part],
        preferred_element_type=jnp.float32,
    )
    pair_acc = jnp.dot(
        lax.all_gather(weight_q, "col", axis=1, tiled=True),
        pair_rows,
        preferred_element_type=jnp.float32,
    )
    ph_acc = jnp.dot(
        lax.all_gather(weight_g, "col", axis=1, tiled=True),
        ph_rows,
        preferred_element_type=jnp.float32,
    )
    pair_grad = jnp.concatenate(
        [2.0 * energy - 2.0 * pair_acc[:, :rank_part], -2.0 * pair_acc[:, rank_part:]], axis=1
    )
    outgoing_back = jnp.take(ph_acc[:, :rank_part], slot_back, axis=0)
    returned = lax.all_to_all(outgoing_back, "row", split_axis=0, concat_axis=0, tiled=True)
    returned = jnp.take(returned, anchor_back, axis=0)
    grad_density = (
        pair_grad[:, :rank_part]
        + 2.0 * scale_rows[:, None] * density_factor.astype(jnp.float32)
        - 2.0 * returned
    )
    grad_hole = pair_grad[:, rank_part:]
    grad_ph = -2.0 * ph_acc[:, rank_part:]
    return (grad_density, grad_hole, grad_ph)


def solution(mesh):
    return jax.shard_map(
        local,
        mesh=mesh,
        in_specs=(
            P("row", "col"),
            P("row", "col"),
            P("row", "col"),
            P("row", "col"),
            P("row", "col"),
            P("row", "col"),
            P(),
            P(),
        ),
        out_specs=(P("row", "col"), P("row", "col"), P("row", "col")),
        check_vma=False,
    )
```

profile of v0, /device:TPU:2, one launch (start us, length us, event | category | flops | bytes accessed | tf_op | source)
XLA Modules:
  0.0 627.2 jit_solution(385054818816971866)
XLA Ops:
  7.2 0.9 copy.38
  8.1 0.9 copy.39
  9.0 0.7 pad_maximum_fusion.1
  9.7 0.8 reshape.102
  10.6 3.7 sort.48
  14.3 0.1 reshape.157
  14.4 1.9 gather_fusion
  16.5 0.1 sub.37
  16.6 0.8 gather_fusion.1
  17.4 0.1 broadcast_select_fusion.2
  17.5 0.7 reshape.214
  18.3 11.6 %all-to-all-start = ((bf16[32,2,192]{2,1,0:T(2,128)(2,1)}), bf16[32,2,192]{2,1,0:T(2,128)(2,1)S(1)}, u32[]{:S(2)}, u32[]{:S(2)}) async-start(bf16[32,2,192]{2,1,0:T(2,128)(2,1)} %reshape.214), calls=%async_computation | async-start | bytes 65536 | tf_op jit(solution)/shard_map/all_to_all | solution.py:77
  30.0 0.6 reduce-window.18
  30.6 0.2 slice_reduce_fusion
  31.0 0.1 copy.43
  31.1 7.4 %all-to-all-done = bf16[32,2,192]{2,1,0:T(2,128)(2,1)S(1)} async-done(((bf16[32,2,192]{2,1,0:T(2,128)(2,1)}), bf16[32,2,192]{2,1,0:T(2,128)(2,1)S(1)}, u32[]{:S(2)}, u32[]{:S(2)}) %all-to-all-start) | async-done | bytes 24608 | tf_op jit(solution)/shard_map/all_to_all | solution.py:77
  38.5 0.1 reshape.215
  38.6 0.8 gather_fusion.2
  39.5 0.7 pad_maximum_fusion.2
  40.3 0.6 dynamic-slice
  41.7 0.2 fusion.22
  41.9 19.4 %all-reduce.5 = (f32[192]{0:T(256)S(1)}, f32[192]{0:T(256)S(1)}, f32[192]{0:T(256)S(1)}) all-reduce(f32[192]{0:T(256)S(1)} %fusion.25, f32[192]{0:T(256)S(1)} %fusion.22, f32[192]{0:T(256)S(1)} %multiply_reduce_fusion), channel_id=1, replica_groups=mesh['row'=32,'col'=8] {'col'}, use_global_device_ids=true, to_apply=%region_10.12 | all-reduce | flops 576 | bytes 4608 | tf_op jit(solution)/shard_map/psum | solution.py:50
  61.4 0.3 dynamic-update-slice
  61.6 0.3 dynamic-update-slice.1
  61.9 0.3 dynamic-update-slice.2
  62.2 0.3 copy-done.13
  62.5 0.3 copy-done.11
  62.9 3.5 all-gather.6.cloned.1.call-done
  66.4 4.3 fusion.35
  70.7 49.3 %all-gather.10.cloned.1.call-done = bf16[6144,128]{1,0:T(8,128)(2,1)} async-done(((bf16[192,128]{1,0:T(8,128)(2,1)}), bf16[6144,128]{1,0:T(8,128)(2,1)}) %all-gather.10.cloned.1.call-update) | async-done | bytes 1572880 | tf_op jit(solution)/shard_map/all_gather | solution.py:82
  120.0 2.3 fusion.36
  122.3 0.5 copy-done.1
  122.8 4.7 pad_maximum_fusion
  127.5 0.6 copy-done.18
  128.3 0.1 reduce.1
  128.4 0.2 convert_reduce_fusion
  128.7 242.1 %all-reduce.8.cloned.1.call-done = (f32[6144]{0:T(1024)}, f32[6144]{0:T(1024)}, f32[6144]{0:T(1024)}) async-done(((f32[6144]{0:T(1024)}, f32[6144]{0:T(1024)}, f32[6144]{0:T(1024)}), (f32[6144]{0:T(1024)}, f32[6144]{0:T(1024)}, f32[6144]{0:T(1024)})) %all-reduce.8.cloned.1.call-update) | async-done | bytes 73744
  370.8 28.4 %gather_fusion.4 = f32[6144]{0:T(1024)S(1)} fusion(f32[6144]{0:T(1024)} %get-tuple-element.24, s32[6144]{0:T(1024)S(1)} %get-tuple-element.43), kind=kCustom, calls=%fused_computation.4.clone | custom fusion | bytes 73728 | tf_op jit(solution)/shard_map/jit(_take)/gather | solution.py:58
  399.2 0.3 select_reduce_fusion.3
  399.5 0.3 select_reduce_fusion.2
  399.8 34.3 %gather_fusion.3 = f32[6144]{0:T(1024)S(1)} fusion(f32[6144]{0:T(1024)S(1)} %broadcast_multiply_fusion, s32[6144]{0:T(1024)S(1)} %get-tuple-element.43), kind=kCustom, calls=%fused_computation.1.clone | custom fusion | bytes 73728 | tf_op jit(solution)/shard_map/jit(_take)/gather | solution.py:57
  434.2 45.5 %reduce-scatter.2.cloned.1.call-done = f32[768,384]{0,1:T(8,128)} async-done(((f32[6144,384]{0,1:T(8,128)}), f32[768,384]{0,1:T(8,128)}) %reduce-scatter.2.cloned.1.call-update) | async-done | bytes 1179664 | tf_op jit(solution)/shard_map/reduce_scatter | solution.py:86
  479.8 2.4 fusion.21
  482.2 0.5 all-gather.12.cloned.1.call-update
  482.8 0.7 all-gather.8.cloned.1.call-update
  483.5 3.2 sort.49
  486.7 3.2 sort.50
  489.9 23.2 %scatter_custom_fusion = f32[6144]{0:T(1024)S(1)} fusion(s32[6144]{0:T(1024)S(1)} %get-tuple-element.42, f32[6144]{0:T(1024)S(1)} %get-tuple-element.30, f32[]{:T(128)} %constant.68.clone.1), kind=kCustom, calls=%fused_computation.76 | custom fusion | bytes 24580 | tf_op jit(solution)/shard_map/scatter | solution.py:59
  513.1 0.3 select_reduce_fusion.1
  513.4 0.3 select_reduce_fusion
  513.7 12.0 %all-gather.14.cloned.1.call-done = bf16[192,6144]{1,0:T(8,128)(2,1)} async-done(((bf16[192,768]{1,0:T(8,128)(2,1)}), bf16[192,6144]{1,0:T(8,128)(2,1)}) %all-gather.14.cloned.1.call-update) | async-done | bytes 2359312 | tf_op jit(solution)/shard_map/all_gather | solution.py:112
  525.7 2.4 fusion.38
  528.2 0.7 gather_fusion.5
  529.1 0.7 reshape.216
  529.8 9.0 %all-to-all-start.1 = ((f32[32,1,384]{2,1,0:T(1,128)}), f32[32,1,384]{2,1,0:T(1,128)S(1)}, u32[]{:S(2)}, u32[]{:S(2)}) async-start(f32[32,1,384]{2,1,0:T(1,128)} %reshape.216), calls=%async_computation.2 | async-start | bytes 98304 | tf_op jit(solution)/shard_map/all_to_all | solution.py:120
  538.8 32.1 %all-gather.12.cloned.1.call-done = bf16[192,6144]{1,0:T(8,128)(2,1)} async-done(((bf16[192,768]{1,0:T(8,128)(2,1)}), bf16[192,6144]{1,0:T(8,128)(2,1)}) %all-gather.12.cloned.1.call-update) | async-done | bytes 2359312 | tf_op jit(solution)/shard_map/all_gather | solution.py:107
  570.9 2.4 fusion.37
  573.5 0.7 copy.47
  574.2 0.7 copy.48
  574.9 0.5 broadcast.144
  575.4 0.8 reduce.3
  576.3 0.7 gather_fusion.6
  577.1 40.1 %all-gather.8.cloned.1.call-done = bf16[192,6144]{1,0:T(8,128)(2,1)} async-done(((bf16[192,768]{1,0:T(8,128)(2,1)}), bf16[192,6144]{1,0:T(8,128)(2,1)}) %all-gather.8.cloned.1.call-update) | async-done | bytes 2359312 | tf_op jit(solution)/shard_map/all_gather | solution.py:102
  617.2 3.1 fusion.14
  (104 shorter events, 2.1 us)
Async XLA Ops:
  7.2 59.2 %all-gather.6.cloned.1.call-start = ((), (), s32[]{:S(2)}) async-start(), calls=%async_computation.3 | async-start | bytes 1622016 | tf_op jit(solution)/shard_map/all_gather | solution.py:81
  14.4 16.6 %copy-start.10 = (bf16[192,64]{0,1:T(8,128)(2,1)S(1)}, bf16[192,64]{0,1:T(8,128)(2,1)}, u32[]{:S(2)}) copy-start(bf16[192,64]{0,1:T(8,128)(2,1)} %param.16) | copy-start | bytes 73732
  16.3 24.0 %copy-start.19 = (u32[256]{0:T(256)S(1)}, u32[256]{0:T(256)}, u32[]{:S(2)}) copy-start(u32[256]{0:T(256)} %constant.123) | copy-start | bytes 3076
  16.3 25.3 %copy-start.7 = (bf16[192,64]{0,1:T(8,128)(2,1)S(1)}, bf16[192,64]{0,1:T(8,128)(2,1)}, u32[]{:S(2)}) copy-start(bf16[192,64]{0,1:T(8,128)(2,1)} %param.14) | copy-start | bytes 73732
  16.3 25.3 %copy-start.4 = (bf16[192,768]{1,0:T(8,128)(2,1)S(1)}, bf16[192,768]{1,0:T(8,128)(2,1)}, u32[]{:S(2)}) copy-start(bf16[192,768]{1,0:T(8,128)(2,1)} %param.19) | copy-start | bytes 884740
  16.4 50.0 %copy-start.5 = (bf16[192,128]{1,0:T(8,128)(2,1)S(1)}, bf16[192,128]{1,0:T(8,128)(2,1)}, u32[]{:S(2)}) copy-start(bf16[192,128]{1,0:T(8,128)(2,1)} %pad_maximum_fusion.1) | copy-start | bytes 147460
  18.3 20.2 %all-to-all-start = ((bf16[32,2,192]{2,1,0:T(2,128)(2,1)}), bf16[32,2,192]{2,1,0:T(2,128)(2,1)S(1)}, u32[]{:S(2)}, u32[]{:S(2)}) async-start(bf16[32,2,192]{2,1,0:T(2,128)(2,1)} %reshape.214), calls=%async_computation | async-start | bytes 65536 | tf_op jit(solution)/shard_map/all_to_all | solution.py:77
  29.9 90.1 %all-gather.10.cloned.1.call-start = ((), (), s32[]{:S(2)}) async-start(), calls=%async_computation.5 | async-start | bytes 1622016 | tf_op jit(solution)/shard_map/all_gather | solution.py:82
  40.3 330.5 %all-reduce.8.cloned.1.call-start = ((), (), s32[]{:S(2)}) async-start(), calls=%async_computation.9 | async-start | bytes 147456
  41.6 20.6 %copy-start.16 = (s32[192]{0:T(256)}, s32[192]{0:T(256)S(1)}, u32[]{:S(2)}) copy-start(s32[192]{0:T(256)S(1)} %iota_add_fusion.2) | copy-start | bytes 2308
  61.6 0.6 copy-start.12
  61.9 0.6 copy-start.13
  62.2 0.6 copy-start.11
  62.8 57.2 %copy-start.6 = (bf16[192,128]{1,0:T(8,128)(2,1)S(1)}, bf16[192,128]{1,0:T(8,128)(2,1)}, u32[]{:S(2)}) copy-start(bf16[192,128]{1,0:T(8,128)(2,1)} %pad_maximum_fusion.2) | copy-start | bytes 147460
  62.8 417.0 %reduce-scatter.2.cloned.1.call-start = ((), (), s32[]{:S(2)}) async-start(), calls=%async_computation.6 | async-start | bytes 10616832 | tf_op jit(solution)/shard_map/reduce_scatter | solution.py:86
  120.0 2.8 copy-start.1
  127.5 0.7 copy-start.18
  127.5 1.2 copy-start.9
  127.5 398.2 %all-gather.14.cloned.1.call-start = ((), (), s32[]{:S(2)}) async-start(), calls=%async_computation.8 | async-start | bytes 2654208 | tf_op jit(solution)/shard_map/all_gather | solution.py:112
  370.8 28.4 %copy-start = (f32[6144]{0:T(1024)S(1)}, f32[6144]{0:T(1024)}, u32[]{:S(2)}) copy-start(f32[6144]{0:T(1024)} %get-tuple-element.24) | copy-start | bytes 73732
  399.7 34.3 %copy-start.14 = (f32[6144]{0:T(1024)S(1)}, f32[6144]{0:T(1024)}, u32[]{:S(2)}) copy-start(f32[6144]{0:T(1024)} %get-tuple-element.25) | copy-start | bytes 73732
  399.8 34.3 %copy-start.15 = (f32[6144]{0:T(1024)S(1)}, f32[6144]{0:T(1024)}, u32[]{:S(2)}) copy-start(f32[6144]{0:T(1024)} %get-tuple-element.26) | copy-start | bytes 73732
  399.8 80.0 %copy-start.8 = (bf16[192,768]{1,0:T(8,128)(2,1)S(1)}, bf16[192,768]{1,0:T(8,128)(2,1)}, u32[]{:S(2)}) copy-start(bf16[192,768]{1,0:T(8,128)(2,1)} %param.18) | copy-start | bytes 884740
  399.8 80.0 %copy-start.17 = (s32[192]{0:T(256)S(1)}, s32[192]{0:T(256)}, u32[]{:S(2)}) copy-start(s32[192]{0:T(256)} %copy-done.16) | copy-start | bytes 2308
  434.2 91.5 %copy-start.3 = (bf16[6144,128]{1,0:T(8,128)(2,1)S(1)}, bf16[6144,128]{1,0:T(8,128)(2,1)}, u32[]{:S(2)}) copy-start(bf16[6144,128]{1,0:T(8,128)(2,1)} %all-gather.10.cloned.1.call-done) | copy-start | bytes 4718596
  482.2 88.7 %all-gather.12.cloned.1.call-start = ((), (), s32[]{:S(2)}) async-start(), calls=%async_computation.7 | async-start | bytes 2654208 | tf_op jit(solution)/shard_map/all_gather | solution.py:107
  482.7 134.5 %all-gather.8.cloned.1.call-start = ((), (), s32[]{:S(2)}) async-start(), calls=%async_computation.4 | async-start | bytes 2654208 | tf_op jit(solution)/shard_map/all_gather | solution.py:102
  528.1 42.7 %copy-start.2 = (bf16[6144,128]{1,0:T(8,128)(2,1)S(1)}, bf16[6144,128]{1,0:T(8,128)(2,1)}, u32[]{:S(2)}) copy-start(bf16[6144,128]{1,0:T(8,128)(2,1)} %all-gather.6.cloned.1.call-done) | copy-start | bytes 4718596
  529.8 45.1 %all-to-all-start.1 = ((f32[32,1,384]{2,1,0:T(1,128)}), f32[32,1,384]{2,1,0:T(1,128)S(1)}, u32[]{:S(2)}, u32[]{:S(2)}) async-start(f32[32,1,384]{2,1,0:T(1,128)} %reshape.216), calls=%async_computation.2 | async-start | bytes 98304 | tf_op jit(solution)/shard_map/all_to_all | solution.py:120
Sparse Core Ops, SparseCore 0:
  11.1 55.2 all-gather.5
  69.5 50.4 all-gather.9
  123.4 247.3 all-reduce.7
  373.4 106.3 reduce-scatter.1
  482.3 43.3 all-gather.13
  527.5 43.3 all-gather.11
  572.8 44.3 all-gather.7
where the time goes:
time: 628 us; the launch traced here: 627 us
  waiting for transfers between devices  433 us (69%)
  local copies, waits for them, and re-layouts  101 us (16%)
  other arithmetic  22.5 us (4%)
  starting transfers between devices  20.9 us (3%)
  blocking collectives  19.4 us (3%)
  between operations  15.3 us (2%)
  matrix products  14.6 us (2%)
    unnamed x8, waiting for transfers between devices  243 us
    all_gather x1, waiting for transfers between devices, local(): lax.all_gather(ph_local, 'row', axis=0, tiled=True)  49.3 us
    reduce_scatter x1, waiting for transfers between devices, local(): lax.psum_scatter(jnp.concatenate([contract_rows(pair_rows, pair_local), c...  45.5 us
    all_gather x1, waiting for transfers between devices, local(): lax.all_gather(hamiltonian, 'col', axis=1, tiled=True)  40.1 us
    gather x1, local copies, waits for them, and re-layouts, local(): shifted_ph = jnp.take(shifted, ph_perm)  34.3 us
    all_gather x1, waiting for transfers between devices, local(): lax.all_gather(weight_q, 'col', axis=1, tiled=True)  32.1 us
    gather x1, local copies, waits for them, and re-layouts, local(): jnp.take(density_all, ph_perm)  28.4 us
    scatter x1, local copies, waits for them, and re-layouts, local(): weight_pair = jnp.zeros_like(weight_diag).at[ph_perm].set(weight_diag)  23.2 us
  transfers between devices with their start and end apart: 9, of which 8 were waited for; matrix products, arithmetic and copies ran while one was open for 20% of the time, Pallas kernels for 0%

commit v1 on v0

--- a/solution.py
+++ b/solution.py
@@ -5,6 +5,13 @@
 
 shift_value = 2.0
 penalty = 2.5
+
+
+def push_the_regions(xx):
+    t1 = jnp.concatenate(
+        lax.all_to_all(jnp.stack([xx] * lax.axis_size("col"), axis=0), "col", 0, 0), axis=1
+    )
+    return t1
 
 
 def block_means(values, lengths):
@@ -103,11 +110,7 @@
         pair_rows[:, :rank_part],
         preferred_element_type=jnp.float32,
     )
-    pair_acc = jnp.dot(
-        lax.all_gather(weight_q, "col", axis=1, tiled=True),
-        pair_rows,
-        preferred_element_type=jnp.float32,
-    )
+    pair_acc = jnp.dot(push_the_regions(weight_q), pair_rows, preferred_element_type=jnp.float32)
     ph_acc = jnp.dot(
         lax.all_gather(weight_g, "col", axis=1, tiled=True),
         ph_rows,

time: 628 us -> 602 us (0.959)
  waiting for transfers between devices: 433 us -> 397 us
  local copies, waits for them, and re-layouts: 101 us -> 108 us
    all_gather x1 -> x0, waiting for transfers between devices: 32.1 us -> none  [local(): lax.all_gather(weight_q, 'col', axis=1, tiled=True)]
    all_gather x1, waiting for transfers between devices: 40.1 us -> 22.2 us  [local(): lax.all_gather(hamiltonian, 'col', axis=1, tiled=True)]
    unnamed x8 -> x7, waiting for transfers between devices: 243 us -> 243 us
  transfers between devices with their start and end apart: 9 -> 9, of which waited for: 8 -> 9; matrix products, arithmetic and copies ran while one was open for 20% -> 22% of each run, Pallas kernels for 0% -> 0%
where the time goes in v1:
time: 602 us; the launch traced here: 601 us
  waiting for transfers between devices  397 us (66%)
  local copies, waits for them, and re-layouts  108 us (18%)
  starting transfers between devices  24.2 us (4%)
  other arithmetic  22.5 us (4%)
  blocking collectives  19.4 us (3%)
  between operations  15.3 us (3%)
  matrix products  14.6 us (2%)
    unnamed x7, waiting for transfers between devices  243 us
    all_gather x1, waiting for transfers between devices, local(): lax.all_gather(ph_local, 'row', axis=0, tiled=True)  49.2 us
    reduce_scatter x1, waiting for transfers between devices, local(): lax.psum_scatter(jnp.concatenate([contract_rows(pair_rows, pair_local), c...  45.5 us
    gather x1, local copies, waits for them, and re-layouts, local(): shifted_ph = jnp.take(shifted, ph_perm)  34.3 us
    gather x1, local copies, waits for them, and re-layouts, local(): jnp.take(density_all, ph_perm)  28.4 us
    scatter x1, local copies, waits for them, and re-layouts, local(): weight_pair = jnp.zeros_like(weight_diag).at[ph_perm].set(weight_diag)  23.2 us
    all_gather x1, waiting for transfers between devices, local(): lax.all_gather(hamiltonian, 'col', axis=1, tiled=True)  22.2 us
    psum x1, blocking collectives, local(): lax.psum((density_sq, ph_sq, mult_diag), 'col')  19.4 us
  transfers between devices with their start and end apart: 9, of which 9 were waited for; matrix products, arithmetic and copies ran while one was open for 22% of the time, Pallas kernels for 0%

profile of v1, /device:TPU:2, one launch (start us, length us, event | category | flops | bytes accessed | tf_op | source)
XLA Modules:
  0.0 600.8 jit_solution(16489496962214085795)
XLA Ops:
  7.2 0.9 copy.39
  8.1 0.9 copy.40
  9.0 0.7 pad_maximum_fusion.1
  9.7 0.8 reshape.110
  10.6 3.7 sort.48
  14.4 1.9 gather_fusion
  16.6 0.8 gather_fusion.1
  17.6 0.7 reshape.224
  18.3 11.6 %all-to-all-start = ((bf16[32,2,192]{2,1,0:T(2,128)(2,1)}), bf16[32,2,192]{2,1,0:T(2,128)(2,1)S(1)}, u32[]{:S(2)}, u32[]{:S(2)}) async-start(bf16[32,2,192]{2,1,0:T(2,128)(2,1)} %reshape.224), calls=%async_computation | async-start | bytes 65536 | tf_op jit(solution)/shard_map/all_to_all | solution.py:84
  30.0 0.6 reduce-window.18
  30.6 0.2 slice_reduce_fusion
  31.0 0.1 copy.44
  31.1 7.4 %all-to-all-done = bf16[32,2,192]{2,1,0:T(2,128)(2,1)S(1)} async-done(((bf16[32,2,192]{2,1,0:T(2,128)(2,1)}), bf16[32,2,192]{2,1,0:T(2,128)(2,1)S(1)}, u32[]{:S(2)}, u32[]{:S(2)}) %all-to-all-start) | async-done | bytes 24608 | tf_op jit(solution)/shard_map/all_to_all | solution.py:84
  38.7 0.8 gather_fusion.2
  39.5 0.7 pad_maximum_fusion.2
  40.3 0.6 dynamic-slice
  41.7 0.2 fusion.22
  41.9 19.4 %all-reduce.5 = (f32[192]{0:T(256)S(1)}, f32[192]{0:T(256)S(1)}, f32[192]{0:T(256)S(1)}) all-reduce(f32[192]{0:T(256)S(1)} %fusion.25, f32[192]{0:T(256)S(1)} %fusion.22, f32[192]{0:T(256)S(1)} %multiply_reduce_fusion), channel_id=1, replica_groups=mesh['row'=32,'col'=8] {'col'}, use_global_device_ids=true, to_apply=%region_10.12 | all-reduce | flops 576 | bytes 4608 | tf_op jit(solution)/shard_map/psum | solution.py:57
  61.4 0.3 dynamic-update-slice
  61.6 0.3 dynamic-update-slice.1
  61.9 0.3 dynamic-update-slice.2
  62.2 0.3 copy-done.14
  62.5 0.3 copy-done.12
  62.9 3.5 all-gather.5.cloned.1.call-done
  66.4 4.4 fusion.35
  70.8 49.2 %all-gather.9.cloned.1.call-done = bf16[6144,128]{1,0:T(8,128)(2,1)} async-done(((bf16[192,128]{1,0:T(8,128)(2,1)}), bf16[6144,128]{1,0:T(8,128)(2,1)}) %all-gather.9.cloned.1.call-update) | async-done | bytes 1572880 | tf_op jit(solution)/shard_map/all_gather | solution.py:89
  120.0 2.3 fusion.36
  122.3 0.5 copy-done.1
  122.8 4.7 pad_maximum_fusion
  127.6 0.6 copy-done.19
  128.3 0.1 reduce.1
  128.5 0.2 convert_reduce_fusion
  128.7 242.1 %all-reduce.8.cloned.1.call-done = (f32[6144]{0:T(1024)}, f32[6144]{0:T(1024)}, f32[6144]{0:T(1024)}) async-done(((f32[6144]{0:T(1024)}, f32[6144]{0:T(1024)}, f32[6144]{0:T(1024)}), (f32[6144]{0:T(1024)}, f32[6144]{0:T(1024)}, f32[6144]{0:T(1024)})) %all-reduce.8.cloned.1.call-update) | async-done | bytes 73744
  370.8 28.4 %gather_fusion.4 = f32[6144]{0:T(1024)S(1)} fusion(f32[6144]{0:T(1024)} %get-tuple-element.24, s32[6144]{0:T(1024)S(1)} %get-tuple-element.43), kind=kCustom, calls=%fused_computation.4.clone | custom fusion | bytes 73728 | tf_op jit(solution)/shard_map/jit(_take)/gather | solution.py:65
  399.2 0.3 select_reduce_fusion.3
  399.5 0.3 select_reduce_fusion.2
  399.8 34.3 %gather_fusion.3 = f32[6144]{0:T(1024)S(1)} fusion(f32[6144]{0:T(1024)S(1)} %broadcast_multiply_fusion, s32[6144]{0:T(1024)S(1)} %get-tuple-element.43), kind=kCustom, calls=%fused_computation.1.clone | custom fusion | bytes 73728 | tf_op jit(solution)/shard_map/jit(_take)/gather | solution.py:64
  434.2 45.5 %reduce-scatter.2.cloned.1.call-done = f32[768,384]{0,1:T(8,128)} async-done(((f32[6144,384]{0,1:T(8,128)}), f32[768,384]{0,1:T(8,128)}) %reduce-scatter.2.cloned.1.call-update) | async-done | bytes 1179664 | tf_op jit(solution)/shard_map/reduce_scatter | solution.py:93
  479.8 2.3 fusion.21
  482.1 1.6 stack.2
  483.7 3.6 all-to-all-start.1
  487.4 0.5 all-gather.7.cloned.1.call-update
  487.9 3.2 sort.49
  491.1 3.2 sort.50
  494.3 23.2 %scatter_custom_fusion = f32[6144]{0:T(1024)S(1)} fusion(s32[6144]{0:T(1024)S(1)} %get-tuple-element.42, f32[6144]{0:T(1024)S(1)} %get-tuple-element.30, f32[]{:T(128)} %constant.68.clone.1), kind=kCustom, calls=%fused_computation.76 | custom fusion | bytes 24580 | tf_op jit(solution)/shard_map/scatter | solution.py:66
  517.5 0.3 select_reduce_fusion.1
  517.8 0.3 select_reduce_fusion
  518.2 6.2 %all-to-all-done.1 = bf16[8,192,768]{2,1,0:T(8,128)(2,1)S(1)} async-done(((bf16[8,192,768]{2,1,0:T(8,128)(2,1)}), bf16[8,192,768]{2,1,0:T(8,128)(2,1)S(1)}, u32[]{:S(2)}, u32[]{:S(2)}) %all-to-all-start.1) | async-done | bytes 2359328 | tf_op jit(solution)/shard_map/all_to_all | solution.py:12
  524.4 1.4 copy-done.4
  525.8 3.5 copy.54
  529.4 15.6 %all-gather.11.cloned.1.call-done = bf16[192,6144]{1,0:T(8,128)(2,1)} async-done(((bf16[192,768]{1,0:T(8,128)(2,1)}), bf16[192,6144]{1,0:T(8,128)(2,1)}) %all-gather.11.cloned.1.call-update) | async-done | bytes 2359312 | tf_op jit(solution)/shard_map/all_gather | solution.py:115
  545.0 2.4 fusion.38
  547.5 0.7 gather_fusion.5
  548.3 0.7 reshape.226
  549.1 8.7 %all-to-all-start.2 = ((f32[32,1,384]{2,1,0:T(1,128)}), f32[32,1,384]{2,1,0:T(1,128)S(1)}, u32[]{:S(2)}, u32[]{:S(2)}) async-start(f32[32,1,384]{2,1,0:T(1,128)} %reshape.226), calls=%async_computation.3 | async-start | bytes 98304 | tf_op jit(solution)/shard_map/all_to_all | solution.py:123
  557.8 2.4 fusion.37
  560.4 0.7 copy.49
  561.1 0.7 copy.50
  561.8 4.7 all-to-all-done.2
  566.5 0.5 broadcast.146
  567.0 0.8 reduce.3
  567.9 0.7 gather_fusion.6
  568.6 22.2 %all-gather.7.cloned.1.call-done = bf16[192,6144]{1,0:T(8,128)(2,1)} async-done(((bf16[192,768]{1,0:T(8,128)(2,1)}), bf16[192,6144]{1,0:T(8,128)(2,1)}) %all-gather.7.cloned.1.call-update) | async-done | bytes 2359312 | tf_op jit(solution)/shard_map/all_gather | solution.py:109
  590.9 3.1 fusion.14
  (107 shorter events, 2.4 us)
Async XLA Ops:
  7.2 59.2 %all-gather.5.cloned.1.call-start = ((), (), s32[]{:S(2)}) async-start(), calls=%async_computation.4 | async-start | bytes 1622016 | tf_op jit(solution)/shard_map/all_gather | solution.py:88
  14.4 16.6 %copy-start.11 = (bf16[192,64]{0,1:T(8,128)(2,1)S(1)}, bf16[192,64]{0,1:T(8,128)(2,1)}, u32[]{:S(2)}) copy-start(bf16[192,64]{0,1:T(8,128)(2,1)} %param.16) | copy-start | bytes 73732
  16.3 24.0 %copy-start.20 = (u32[256]{0:T(256)S(1)}, u32[256]{0:T(256)}, u32[]{:S(2)}) copy-start(u32[256]{0:T(256)} %constant.123) | copy-start | bytes 3076
  16.3 25.3 %copy-start.8 = (bf16[192,64]{0,1:T(8,128)(2,1)S(1)}, bf16[192,64]{0,1:T(8,128)(2,1)}, u32[]{:S(2)}) copy-start(bf16[192,64]{0,1:T(8,128)(2,1)} %param.14) | copy-start | bytes 73732
  16.3 25.3 %copy-start.5 = (bf16[192,768]{1,0:T(8,128)(2,1)S(1)}, bf16[192,768]{1,0:T(8,128)(2,1)}, u32[]{:S(2)}) copy-start(bf16[192,768]{1,0:T(8,128)(2,1)} %param.19) | copy-start | bytes 884740
  16.4 50.0 %copy-start.6 = (bf16[192,128]{1,0:T(8,128)(2,1)S(1)}, bf16[192,128]{1,0:T(8,128)(2,1)}, u32[]{:S(2)}) copy-start(bf16[192,128]{1,0:T(8,128)(2,1)} %pad_maximum_fusion.1) | copy-start | bytes 147460
  18.3 20.2 %all-to-all-start = ((bf16[32,2,192]{2,1,0:T(2,128)(2,1)}), bf16[32,2,192]{2,1,0:T(2,128)(2,1)S(1)}, u32[]{:S(2)}, u32[]{:S(2)}) async-start(bf16[32,2,192]{2,1,0:T(2,128)(2,1)} %reshape.224), calls=%async_computation | async-start | bytes 65536 | tf_op jit(solution)/shard_map/all_to_all | solution.py:84
  29.9 90.1 %all-gather.9.cloned.1.call-start = ((), (), s32[]{:S(2)}) async-start(), calls=%async_computation.6 | async-start | bytes 1622016 | tf_op jit(solution)/shard_map/all_gather | solution.py:89
  40.3 330.5 %all-reduce.8.cloned.1.call-start = ((), (), s32[]{:S(2)}) async-start(), calls=%async_computation.9 | async-start | bytes 147456
  41.6 20.6 %copy-start.17 = (s32[192]{0:T(256)}, s32[192]{0:T(256)S(1)}, u32[]{:S(2)}) copy-start(s32[192]{0:T(256)S(1)} %iota_add_fusion.2) | copy-start | bytes 2308
  61.6 0.6 copy-start.13
  61.9 0.6 copy-start.14
  62.2 0.6 copy-start.12
  62.8 57.2 %copy-start.7 = (bf16[192,128]{1,0:T(8,128)(2,1)S(1)}, bf16[192,128]{1,0:T(8,128)(2,1)}, u32[]{:S(2)}) copy-start(bf16[192,128]{1,0:T(8,128)(2,1)} %pad_maximum_fusion.2) | copy-start | bytes 147460
  62.8 417.0 %reduce-scatter.2.cloned.1.call-start = ((), (), s32[]{:S(2)}) async-start(), calls=%async_computation.7 | async-start | bytes 10616832 | tf_op jit(solution)/shard_map/reduce_scatter | solution.py:93
  120.0 2.8 copy-start.1
  127.5 0.7 copy-start.19
  127.5 1.2 copy-start.10
  127.6 417.4 %all-gather.11.cloned.1.call-start = ((), (), s32[]{:S(2)}) async-start(), calls=%async_computation.8 | async-start | bytes 2654208 | tf_op jit(solution)/shard_map/all_gather | solution.py:115
  370.8 28.4 %copy-start = (f32[6144]{0:T(1024)S(1)}, f32[6144]{0:T(1024)}, u32[]{:S(2)}) copy-start(f32[6144]{0:T(1024)} %get-tuple-element.24) | copy-start | bytes 73732
  399.8 34.3 %copy-start.15 = (f32[6144]{0:T(1024)S(1)}, f32[6144]{0:T(1024)}, u32[]{:S(2)}) copy-start(f32[6144]{0:T(1024)} %get-tuple-element.25) | copy-start | bytes 73732
  399.8 34.3 %copy-start.16 = (f32[6144]{0:T(1024)S(1)}, f32[6144]{0:T(1024)}, u32[]{:S(2)}) copy-start(f32[6144]{0:T(1024)} %get-tuple-element.26) | copy-start | bytes 73732
  399.8 80.0 %copy-start.9 = (bf16[192,768]{1,0:T(8,128)(2,1)S(1)}, bf16[192,768]{1,0:T(8,128)(2,1)}, u32[]{:S(2)}) copy-start(bf16[192,768]{1,0:T(8,128)(2,1)} %param.18) | copy-start | bytes 884740
  399.8 80.0 %copy-start.18 = (s32[192]{0:T(256)S(1)}, s32[192]{0:T(256)}, u32[]{:S(2)}) copy-start(s32[192]{0:T(256)} %copy-done.17) | copy-start | bytes 2308
  483.7 40.7 %all-to-all-start.1 = ((bf16[8,192,768]{2,1,0:T(8,128)(2,1)}), bf16[8,192,768]{2,1,0:T(8,128)(2,1)S(1)}, u32[]{:S(2)}, u32[]{:S(2)}) async-start(bf16[8,192,768]{2,1,0:T(8,128)(2,1)} %stack.2), calls=%async_computation.2 | async-start | bytes 4718592 | tf_op jit(solution)/shard_map/all_to_all | solution.py:12
  487.3 103.5 %all-gather.7.cloned.1.call-start = ((), (), s32[]{:S(2)}) async-start(), calls=%async_computation.5 | async-start | bytes 2654208 | tf_op jit(solution)/shard_map/all_gather | solution.py:109
  524.4 1.4 copy-start.4
  525.8 19.2 %copy-start.3 = (bf16[6144,128]{1,0:T(8,128)(2,1)S(1)}, bf16[6144,128]{1,0:T(8,128)(2,1)}, u32[]{:S(2)}) copy-start(bf16[6144,128]{1,0:T(8,128)(2,1)} %all-gather.9.cloned.1.call-done) | copy-start | bytes 4718596
  547.4 10.4 %copy-start.2 = (bf16[6144,128]{1,0:T(8,128)(2,1)S(1)}, bf16[6144,128]{1,0:T(8,128)(2,1)}, u32[]{:S(2)}) copy-start(bf16[6144,128]{1,0:T(8,128)(2,1)} %all-gather.5.cloned.1.call-done) | copy-start | bytes 4718596
  549.1 17.4 %all-to-all-start.2 = ((f32[32,1,384]{2,1,0:T(1,128)}), f32[32,1,384]{2,1,0:T(1,128)S(1)}, u32[]{:S(2)}, u32[]{:S(2)}) async-start(f32[32,1,384]{2,1,0:T(1,128)} %reshape.226), calls=%async_computation.3 | async-start | bytes 98304 | tf_op jit(solution)/shard_map/all_to_all | solution.py:123
Sparse Core Ops, SparseCore 0:
  11.1 55.2 all-gather.4
  69.5 50.4 all-gather.8
  123.4 247.3 all-reduce.7
  373.4 106.3 reduce-scatter.1
  482.2 62.7 all-gather.10
  546.8 44.0 all-gather.6
